TPU v7x, 32 devices: a whole 2x2x4 slice. The times are simulated.
32 devices in a mesh: seq: 8 (over z, y), dp: 4 (over x, core).
Axes of the slice: x: 2, y: 2, z: 4, core: 2. Of those that a mesh axis runs over, the one named last changes fastest.
Arguments:
- block_input: bfloat16 [4, 1024, 1536], P('dp', 'seq'), may hold values from -6 to 6
- query_proj: bfloat16 [4, 1024, 768], P('dp', 'seq'), may hold values from -8 to 8
- key_proj: bfloat16 [4, 1024, 768], P('dp', 'seq'), may hold values from -8 to 8
- value_proj: bfloat16 [4, 1024, 768], P('dp', 'seq'), may hold values from -6 to 6
- lengths: int32 [4], P('dp'), may hold values from 256 to 1024, as said below
- out_proj: bfloat16 [1536, 768], replicated, may hold values from -0.21875 to 0.21875
- kernel: float32 [31, 1536], replicated, may hold values from -1 to 1
- conv_bias: float32 [1536], replicated, may hold values from -3 to 3
- grad_output: bfloat16 [4, 1024, 1536], P('dp', 'seq'), may hold values from -6 to 6
Outputs:
- block_output: bfloat16 [4, 1024, 1536], P('dp', 'seq')
- grad_input: bfloat16 [4, 1024, 1536], P('dp', 'seq')
- grad_query: bfloat16 [4, 1024, 768], P('dp', 'seq')
- grad_out_proj: float32 [1536, 768], P('seq')
- grad_kernel: float32 [31, 1536], P(None, 'seq')
- grad_bias: float32 [1536], P('seq')
Inputs may be any that keep to these rules, and one draw needn't show every extreme that they name: `lengths`: frames at or after an utterance's length are padding; in every draw at least one utterance has all 1024 frames valid.
All inputs are finite; a program needn't handle non-finite values.
Results may differ from a plain program's by a relative error of at most 0.012.
The roundings to bfloat16 on the way count: a program that leaves them out, or rounds other values in their place, can miss the bound.
Values may be sent and summed in bfloat16 or wider, within the bound.
No kernel may reach another device: no remote copies, remote signals or barrier semaphores. Data moves between devices by JAX's collectives and lax.ppermute only.
A program may use at most 128 MiB of HBM per device.

v0:
```python
import math
import jax
import jax.numpy as jnp
from jax import lax
from jax.sharding import PartitionSpec as P

D = 1536
H = 8
HS = 96
KW = 31
HD = 768


def with_halo(x, sides, width):
    for axis, dim in sides:
        size, length = (lax.axis_size(axis), x.shape[dim])
        up = [(i, (i + 1) % size) for i in range(size - 1)]
        down = [(j, i) for i, j in up]
        last = lax.slice_in_dim(x, length - width, length, axis=dim)
        leading = lax.slice_in_dim(x, 0, width, axis=dim)
        before = lax.ppermute(last, axis, up)
        after = lax.ppermute(leading, axis, down)
        x = jnp.concatenate([before, x, after], axis=dim)
    return x


def forward_rows(query_one, key_one, value_one, key_valid, score_scale):
    row_total = query_one.shape[0]
    block_rows = math.gcd(row_total, 512)
    query_blocks = query_one.reshape(row_total // block_rows, block_rows, query_one.shape[1])

    def forward_one_block(query_block):
        scores = (
            lax.dot_general(
                query_block, key_one, (((1,), (1,)), ((), ())), preferred_element_type=jnp.float32
            )
            * score_scale
        )
        scores = jnp.where(key_valid[None, :], scores, -jnp.inf)
        row_top = jnp.max(scores, axis=-1, keepdims=True)
        log_total = row_top + jnp.log(jnp.sum(jnp.exp(scores - row_top), axis=-1, keepdims=True))
        weights = jnp.exp(scores - log_total).astype(jnp.bfloat16)
        return (jnp.dot(weights, value_one, preferred_element_type=jnp.float32), log_total[:, 0])

    outputs, log_totals = lax.map(forward_one_block, query_blocks)
    return (outputs.reshape(row_total, query_one.shape[1]), log_totals.reshape(row_total))


def backward_rows(
    query_one, key_one, value_one, grad_one, lse_one, delta_one, key_valid, score_scale
):
    row_total = query_one.shape[0]
    block_rows = math.gcd(row_total, 512)
    block_count = row_total // block_rows
    width = query_one.shape[1]

    def backward_one_block(items):
        query_block, grad_block, lse_block, delta_block = items
        scores = (
            lax.dot_general(
                query_block, key_one, (((1,), (1,)), ((), ())), preferred_element_type=jnp.float32
            )
            * score_scale
        )
        scores = jnp.where(key_valid[None, :], scores, -jnp.inf)
        probs = jnp.exp(scores - lse_block[:, None])
        grad_prob = lax.dot_general(
            grad_block, value_one, (((1,), (1,)), ((), ())), preferred_element_type=jnp.float32
        )
        grad_score = (probs * (grad_prob - delta_block[:, None])).astype(jnp.bfloat16)
        return jnp.dot(grad_score, key_one, preferred_element_type=jnp.float32) * score_scale

    results = lax.map(
        backward_one_block,
        (
            query_one.reshape(block_count, block_rows, width),
            grad_one.reshape(block_count, block_rows, width),
            lse_one.reshape(block_count, block_rows),
            delta_one.reshape(block_count, block_rows),
        ),
    )
    return results.reshape(row_total, width)


def on_device(
    block_input, query_proj, key_proj, value_proj, lengths, out_proj, kernel, conv_bias, grad_output
):
    frames_dev = block_input.shape[1]
    seq_count = lax.axis_size("seq")
    total_frames = frames_dev * seq_count
    first_frame = lax.axis_index("seq") * frames_dev
    utt_length = lengths[0]
    local_valid = first_frame + jnp.arange(frames_dev) < utt_length
    all_valid = jnp.arange(total_frames) < utt_length
    score_scale = 1.0 / math.sqrt(HS)
    halo_width = KW // 2
    group_size = seq_count // H
    sub_rows = frames_dev // group_size
    query_local = query_proj[0]

    def to_serving(matrix):
        return matrix.reshape(frames_dev, H, HS).transpose(1, 0, 2).reshape(seq_count, sub_rows, HS)

    def from_serving(returned):
        return returned.reshape(H, frames_dev, HS).transpose(1, 0, 2).reshape(frames_dev, HD)

    query_mine = lax.all_to_all(
        to_serving(query_local), "seq", split_axis=0, concat_axis=1, tiled=True
    )[0]
    key_send = jnp.repeat(
        key_proj[0].reshape(frames_dev, H, HS).transpose(1, 0, 2), group_size, axis=0
    )
    value_send = jnp.repeat(
        value_proj[0].reshape(frames_dev, H, HS).transpose(1, 0, 2), group_size, axis=0
    )
    key_mine, value_mine = (
        lax.all_to_all(key_send, "seq", split_axis=0, concat_axis=1, tiled=True),
        lax.all_to_all(value_send, "seq", split_axis=0, concat_axis=1, tiled=True),
    )
    key_mine = key_mine[0]
    value_mine = value_mine[0]
    head_out, head_lse = forward_rows(query_mine, key_mine, value_mine, all_valid, score_scale)
    head_attended = head_out.astype(jnp.bfloat16)
    attended = from_serving(
        lax.all_to_all(head_attended[None], "seq", split_axis=1, concat_axis=0, tiled=True)
    )
    projected = lax.dot_general(
        attended, out_proj, (((1,), (1,)), ((), ())), preferred_element_type=jnp.float32
    )
    mixed_rows = (block_input[0].astype(jnp.float32) + projected).astype(jnp.bfloat16)
    masked = jnp.where(local_valid[:, None], mixed_rows, jnp.zeros_like(mixed_rows))
    padded = with_halo(masked, (("seq", 0),), halo_width).astype(jnp.float32)
    conv_rows = jnp.broadcast_to(conv_bias, (frames_dev, D))
    for tap in range(KW):
        conv_rows = conv_rows + kernel[tap] * padded[tap : tap + frames_dev]
    gate_rows = jax.nn.sigmoid(conv_rows)
    block_output = jnp.where(
        local_valid[:, None], mixed_rows.astype(jnp.float32) + conv_rows * gate_rows, 0.0
    ).astype(jnp.bfloat16)
    grad_rows = jnp.where(local_valid[:, None], grad_output[0].astype(jnp.float32), 0.0)
    grad_conv = grad_rows * gate_rows * (1.0 + conv_rows * (1.0 - gate_rows))
    kernel_local = jnp.stack(
        [jnp.sum(grad_conv * padded[tap : tap + frames_dev], axis=0) for tap in range(KW)]
    )
    bias_local = jnp.sum(grad_conv, axis=0)
    grad_padded = with_halo(grad_conv, (("seq", 0),), halo_width)
    grad_masked = jnp.zeros((frames_dev, D), jnp.float32)
    for tap in range(KW):
        begin = 2 * halo_width - tap
        grad_masked = grad_masked + kernel[tap] * grad_padded[begin : begin + frames_dev]
    grad_input = (grad_rows + jnp.where(local_valid[:, None], grad_masked, 0.0)).astype(
        jnp.bfloat16
    )
    grad_attn = jnp.dot(grad_input, out_proj, preferred_element_type=jnp.float32).astype(
        jnp.bfloat16
    )
    grad_mine = lax.all_to_all(
        to_serving(grad_attn), "seq", split_axis=0, concat_axis=1, tiled=True
    )[0]
    delta_mine = jnp.sum(grad_mine.astype(jnp.float32) * head_attended.astype(jnp.float32), axis=-1)
    grad_q_mine = backward_rows(
        query_mine, key_mine, value_mine, grad_mine, head_lse, delta_mine, all_valid, score_scale
    ).astype(jnp.bfloat16)
    grad_query = from_serving(
        lax.all_to_all(grad_q_mine[None], "seq", split_axis=1, concat_axis=0, tiled=True)
    )
    term_block = lax.dot_general(
        grad_input, attended, (((0,), (0,)), ((), ())), preferred_element_type=jnp.float32
    )
    partial_rows = lax.psum_scatter(term_block, "seq", scatter_dimension=0, tiled=True)
    summed = lax.psum(partial_rows.astype(jnp.bfloat16), "dp").astype(jnp.float32)
    kernel_total, bias_total = lax.psum((kernel_local, bias_local), ("seq", "dp"))
    shard_width = D // seq_count
    offset = lax.axis_index("seq") * shard_width
    grad_kernel = lax.dynamic_slice_in_dim(kernel_total, offset, shard_width, 1)
    grad_bias = lax.dynamic_slice_in_dim(bias_total, offset, shard_width, 0)
    return (block_output[None], grad_input[None], grad_query[None], summed, grad_kernel, grad_bias)


def solution(mesh):
    placed = (
        P("dp", "seq", None),
        P("dp", "seq", None),
        P("dp", "seq", None),
        P("dp", "seq", None),
        P("dp"),
        P(),
        P(),
        P(),
        P("dp", "seq", None),
    )
    return jax.shard_map(
        on_device,
        mesh=mesh,
        in_specs=placed,
        out_specs=(
            P("dp", "seq", None),
            P("dp", "seq", None),
            P("dp", "seq", None),
            P("seq", None),
            P(None, "seq"),
            P("seq"),
        ),
        check_vma=False,
    )
```

profile of v0, /device:TPU:0, one launch (start us, length us, event | category | flops | bytes accessed | tf_op | source)
XLA Modules:
  0.0 321.5 jit_solution(12944451114000263372)
XLA Ops:
  9.9 7.3 %all-to-all-start = ((bf16[8,128,96]{1,2,0:T(8,128)(2,1)}), bf16[8,128,96]{1,2,0:T(8,128)(2,1)S(1)}, u32[]{:S(2)}, u32[]{:S(2)}) async-start(bf16[8,128,96]{1,2,0:T(8,128)(2,1)} %bitcast.3), calls=%async_computation | async-start | bytes 393216 | tf_op jit(solution)/shard_map/all_to_all | solution.py:107
  18.9 6.2 %all-to-all-done = bf16[8,128,96]{1,2,0:T(8,128)(2,1)S(1)} async-done(((bf16[8,128,96]{1,2,0:T(8,128)(2,1)}), bf16[8,128,96]{1,2,0:T(8,128)(2,1)S(1)}, u32[]{:S(2)}, u32[]{:S(2)}) %all-to-all-start) | async-done | bytes 196640 | tf_op jit(solution)/shard_map/all_to_all | solution.py:107
  25.1 3.4 %all-to-all-start.1 = ((bf16[8,128,96]{1,2,0:T(8,128)(2,1)}), bf16[8,128,96]{1,2,0:T(8,128)(2,1)S(1)}, u32[]{:S(2)}, u32[]{:S(2)}) async-start(bf16[8,128,96]{1,2,0:T(8,128)(2,1)} %bitcast.5), calls=%async_computation.1 | async-start | bytes 393216 | tf_op jit(solution)/shard_map/all_to_all | solution.py:117
  30.3 6.0 %all-to-all-done.1 = bf16[8,128,96]{1,2,0:T(8,128)(2,1)S(1)} async-done(((bf16[8,128,96]{1,2,0:T(8,128)(2,1)}), bf16[8,128,96]{1,2,0:T(8,128)(2,1)S(1)}, u32[]{:S(2)}, u32[]{:S(2)}) %all-to-all-start.1) | async-done | bytes 196640 | tf_op jit(solution)/shard_map/all_to_all | solution.py:117
  36.3 3.4 %all-to-all-start.2 = ((bf16[8,128,96]{1,2,0:T(8,128)(2,1)}), bf16[8,128,96]{1,2,0:T(8,128)(2,1)S(1)}, u32[]{:S(2)}, u32[]{:S(2)}) async-start(bf16[8,128,96]{1,2,0:T(8,128)(2,1)} %bitcast.7), calls=%async_computation.2 | async-start | bytes 393216 | tf_op jit(solution)/shard_map/all_to_all | solution.py:118
  40.0 7.3 %all-to-all-done.2 = bf16[8,128,96]{1,2,0:T(8,128)(2,1)S(1)} async-done(((bf16[8,128,96]{1,2,0:T(8,128)(2,1)}), bf16[8,128,96]{1,2,0:T(8,128)(2,1)S(1)}, u32[]{:S(2)}, u32[]{:S(2)}) %all-to-all-start.2) | async-done | bytes 196640 | tf_op jit(solution)/shard_map/all_to_all | solution.py:118
  47.6 4.6 %while.24 = (s32[]{:T(128)}, bf16[2,512,96]{1,2,0:T(8,128)(2,1)S(1)}, f32[2,512]{1,0:T(2,128)S(1)}, bf16[2,512,96]{2,1,0:T(8,128)(2,1)S(1)}, bf16[1024,96]{1,0:T...) while((s32[]{:T(128)}, ...), condition=%wide.region_3.4_spmd.clone, body=%wide.region_0.3_spmd.clone.sunk | while | flops 204997120 | bytes 7164021 | solution.py:45
  53.2 2.6 reshape.122
  56.3 3.7 %reduce.63 = bf16[1024,96]{1,0:T(8,128)(2,1)} reduce(bf16[1024,1,96]{2,1,0:T(2,128)(2,1)} %bitcast.115, bf16[]{:T(256)} %broadcast.73), dimensions={1}, to_apply=%bitcast.66.reduce_sub_computation | reduce | bytes 393218
  62.1 3.4 %all-to-all-start.3 = ((bf16[8,2,6144]{2,1,0:T(2,128)(2,1)}), bf16[8,2,6144]{2,1,0:T(2,128)(2,1)S(1)}, u32[]{:S(2)}, u32[]{:S(2)}) async-start(bf16[8,2,6144]{2,1,0:T(2,128)(2,1)} %reshape.155), calls=%async_computation.3 | async-start | bytes 393216 | tf_op jit(solution)/shard_map/all_to_all | solution.py:125
  66.8 2.5 slice_reduce_fusion.30
  69.3 3.9 %all-to-all-done.3 = bf16[8,2,6144]{2,1,0:T(2,128)(2,1)S(1)} async-done(((bf16[8,2,6144]{2,1,0:T(2,128)(2,1)}), bf16[8,2,6144]{2,1,0:T(2,128)(2,1)S(1)}, u32[]{:S(2)}, u32[]{:S(2)}) %all-to-all-start.3) | async-done | bytes 196640 | tf_op jit(solution)/shard_map/all_to_all | solution.py:125
  75.9 2.7 broadcast_select_fusion
  83.5 3.0 collective-permute-done.1
  86.9 7.5 %multiply_reduce_fusion = (f32[1536]{0:T(1024)}, f32[1536]{0:T(1024)}, f32[1536]{0:T(1024)}, f32[1536]{0:T(1024)}, f32[1536]{0:T(1024)}, /*index=5*/f32[1536]{0:...) fusion(f32[158,1536]{1,0:T(8,128)S(1)} %maximum_convert_fusion,, ...), kind=kLoop, calls=%fused_computation.190 | loop fusion | flops 21206016 | bytes 26652800 | tf_op jit(solution)/shard_map/reduce_sum | solution.py:143
  95.7 5.0 %collective-permute-start.3 = (f32[15,1536]{1,0:T(8,128)S(1)}, f32[15,1536]{1,0:T(8,128)S(1)}, u32[]{:S(2)}, u32[]{:S(2)}) collective-permute-start(f32[15,1536]{1,0:T(8,128)S(1)} %get-tuple-element.306), channel_id=1, source_target_pairs={{0,4},{4,8},{8,12},{12,16},{16,20},{20,24},{24,28},{1,5},{5,9},{9,... | collective-permute-start | bytes 276488 | tf_op jit(solution)/shard_map/ppermute | solution.py:21
  102.7 3.7 %fusion.37 = bf16[128,1536]{1,0:T(8,128)(2,1)S(1)} fusion(f32[128,1536]{1,0:T(8,128)S(1)} %get-tuple-element.299, f32[15,1536]{1,0:T(8,128)S(1)} %collective-permute-done.3, f32[15,1536]{1,0:T(8,128)S(1)} %collective-permute-done.2, bf16[1,128,1536]{2,1,0:T(8,128)(2,1)S(1)} %copy-done.11, f32[1536]{0:T(1024)S(1)} %get-tuple-element.265, ...), kind=kLoop, calls=%fused_computation.100 | loop fusion | flops 18874368 | bytes 1947776 | tf_op jit(solution)/shard_map/convert_element_type | solution.py:151
  107.2 2.9 fusion.130
  111.1 2.1 reshape.121
  115.5 6.7 %all-to-all-start.4 = ((bf16[8,128,96]{1,2,0:T(8,128)(2,1)}), bf16[8,128,96]{1,2,0:T(8,128)(2,1)S(1)}, u32[]{:S(2)}, u32[]{:S(2)}) async-start(bf16[8,128,96]{1,2,0:T(8,128)(2,1)} %bitcast.121), calls=%async_computation.4 | async-start | bytes 393216 | tf_op jit(solution)/shard_map/all_to_all | solution.py:157
  122.4 3.0 multiply_reduce_fusion.18
  128.9 3.5 %stack.127 = f32[31,1536]{1,0:T(8,128)} concatenate(f32[1,1536]{1,0:T(1,128)} %stack.96, f32[1,1536]{1,0:T(1,128)} %stack.97, f32[1,1536]{1,0:T(1,128)} %stack.98, f32[1,1536]{1,0:T(1,128)} %stack.99, f32[1,1536]{1,0:T(1,128)} %stack.100, f32[1,1536]{1,0:T(1,128)S(1)} %stack.101, f32[1,1536]{1,0:T(1,128)S(1)} %stack.102, f32[1,1536]{1,0:T(1,128)S(1)} %stack.103, ...), dimensions={0} | concatenate | bytes 380928 | tf_op jit(solution)/shard_map/stack | solution.py:142
  136.5 12.9 %while.25 = (s32[]{:T(128)}, bf16[2,512,96]{1,2,0:T(8,128)(2,1)}, bf16[2,512,96]{2,1,0:T(8,128)(2,1)S(1)}, bf16[1024,96]{1,0:T(8,128)(2,1)S(1)}, f32[2,512]{1,0:...) while((s32[]{:T(128)}, bf16[2,512,96]{1,2,0:T(8,128)(2,1)}, ...), condition=%wide.region_6.7_spmd.clone, body=%wide.region_5.6_spmd.clone.sunk | while | flops 305185792 | bytes 6241429 | solution.py:73
  139.8 3.3 %fusion.163 = bf16[2,512,96]{1,2,0:T(8,128)(2,1)} fusion(bf16[2,512,96]{1,2,0:T(8,128)(2,1)} %get-tuple-element.455, s32[]{:T(128)S(6)} %copy.133, bf16[1024,96]{1,0:T(8,128)(2,1)S(1)} %get-tuple-element.467, f32[512,1024]{1,0:T(8,128)} %fusion.162, bf16[1024,96]{1,0:T(8,128)(2,1)S(1)} %get-tuple-element.470, f32[512]{0:T(512)S(1)} %bitcast.129, ...), kind=kOutput, calls=%fused_computation.17.clone.1 | convolution fusion | flops 204521472 | bytes 2955264 | tf_op jit(solution)/shard_map/while/body/eval_jaxpr/dot_general | solution.py:71
  146.2 3.2 fusion.163
  151.3 2.7 reshape.123
  154.0 3.7 %reduce.64 = bf16[1024,96]{1,0:T(8,128)(2,1)} reduce(bf16[1024,1,96]{2,1,0:T(2,128)(2,1)} %bitcast.116, bf16[]{:T(256)} %broadcast.73), dimensions={1}, to_apply=%bitcast.68.reduce_sub_computation | reduce | bytes 393218
  159.8 4.5 %all-to-all-start.5 = ((bf16[8,2,6144]{2,1,0:T(2,128)(2,1)}), bf16[8,2,6144]{2,1,0:T(2,128)(2,1)}, u32[]{:S(2)}, u32[]{:S(2)}) async-start(bf16[8,2,6144]{2,1,0:T(2,128)(2,1)} %reshape.157), calls=%async_computation.5 | async-start | bytes 393216 | tf_op jit(solution)/shard_map/all_to_all | solution.py:165
  164.3 48.2 %reduce-scatter.2.cloned.1.call-done = f32[192,768]{1,0:T(8,128)} async-done(((f32[1536,768]{1,0:T(8,128)}), f32[192,768]{1,0:T(8,128)}) %reduce-scatter.2.cloned.1.call-update) | async-done | bytes 589840 | tf_op jit(solution)/shard_map/reduce_scatter | solution.py:170
  215.4 40.3 %psum.23 = f32[1536]{0:T(1024)S(1)} all-reduce(f32[1536]{0:T(1024)S(1)} %copy-done.48), channel_id=1, replica_groups=mesh['seq'=8,'dp'=4] {'seq','dp'}, use_global_device_ids=true, to_apply=%region_42.43 | all-reduce | flops 1536 | bytes 12288 | tf_op jit(solution)/shard_map/psum | solution.py:172
  256.4 20.2 %all-reduce.5.cloned.1.call-done = f32[31,1536]{1,0:T(8,128)} async-done(((f32[31,1536]{1,0:T(8,128)}), f32[31,1536]{1,0:T(8,128)}) %all-reduce.5.cloned.1.call-update) | async-done | bytes 190480 | tf_op jit(solution)/shard_map/psum | solution.py:172
  280.6 31.7 %all-reduce.3.cloned.1.call-done = bf16[192,768]{1,0:T(8,128)(2,1)} async-done(((bf16[192,768]{1,0:T(8,128)(2,1)}), bf16[192,768]{1,0:T(8,128)(2,1)}) %all-reduce.3.cloned.1.call-update) | async-done | bytes 294928 | tf_op jit(solution)/shard_map/psum | solution.py:171
  (210 shorter events, 56.5 us)
Async XLA Ops:
  8.0 67.7 %copy-start = (bf16[1536,768]{1,0:T(8,128)(2,1)S(1)}, bf16[1536,768]{1,0:T(8,128)(2,1)}, u32[]{:S(2)}) copy-start(bf16[1536,768]{1,0:T(8,128)(2,1)} %param.18) | copy-start | bytes 7077892
  9.9 15.2 %all-to-all-start = ((bf16[8,128,96]{1,2,0:T(8,128)(2,1)}), bf16[8,128,96]{1,2,0:T(8,128)(2,1)S(1)}, u32[]{:S(2)}, u32[]{:S(2)}) async-start(bf16[8,128,96]{1,2,0:T(8,128)(2,1)} %bitcast.3), calls=%async_computation | async-start | bytes 393216 | tf_op jit(solution)/shard_map/all_to_all | solution.py:107
  25.1 11.1 %all-to-all-start.1 = ((bf16[8,128,96]{1,2,0:T(8,128)(2,1)}), bf16[8,128,96]{1,2,0:T(8,128)(2,1)S(1)}, u32[]{:S(2)}, u32[]{:S(2)}) async-start(bf16[8,128,96]{1,2,0:T(8,128)(2,1)} %bitcast.5), calls=%async_computation.1 | async-start | bytes 393216 | tf_op jit(solution)/shard_map/all_to_all | solution.py:117
  36.3 11.1 %all-to-all-start.2 = ((bf16[8,128,96]{1,2,0:T(8,128)(2,1)}), bf16[8,128,96]{1,2,0:T(8,128)(2,1)S(1)}, u32[]{:S(2)}, u32[]{:S(2)}) async-start(bf16[8,128,96]{1,2,0:T(8,128)(2,1)} %bitcast.7), calls=%async_computation.2 | async-start | bytes 393216 | tf_op jit(solution)/shard_map/all_to_all | solution.py:118
  52.2 14.0 %copy-start.49 = (f32[2,512]{1,0:T(2,128)}, f32[2,512]{1,0:T(2,128)S(1)}, u32[]{:S(2)}) copy-start(f32[2,512]{1,0:T(2,128)S(1)} %get-tuple-element.448) | copy-start | bytes 12292
  52.3 23.3 %copy-start.1 = (bf16[1024,96]{1,0:T(8,128)(2,1)}, bf16[1024,96]{1,0:T(8,128)(2,1)S(1)}, u32[]{:S(2)}) copy-start(bf16[1024,96]{1,0:T(8,128)(2,1)S(1)} %get-tuple-element.477) | copy-start | bytes 589828
  52.3 23.3 %copy-start.3 = (bf16[1024,96]{1,0:T(8,128)(2,1)}, bf16[1024,96]{1,0:T(8,128)(2,1)S(1)}, u32[]{:S(2)}) copy-start(bf16[1024,96]{1,0:T(8,128)(2,1)S(1)} %get-tuple-element.480) | copy-start | bytes 589828
  52.3 23.3 %copy-start.5 = (bf16[2,512,96]{2,1,0:T(8,128)(2,1)}, bf16[2,512,96]{2,1,0:T(8,128)(2,1)S(1)}, u32[]{:S(2)}) copy-start(bf16[2,512,96]{2,1,0:T(8,128)(2,1)S(1)} %get-tuple-element.481) | copy-start | bytes 589828
  62.1 11.1 %all-to-all-start.3 = ((bf16[8,2,6144]{2,1,0:T(2,128)(2,1)}), bf16[8,2,6144]{2,1,0:T(2,128)(2,1)S(1)}, u32[]{:S(2)}, u32[]{:S(2)}) async-start(bf16[8,2,6144]{2,1,0:T(2,128)(2,1)} %reshape.155), calls=%async_computation.3 | async-start | bytes 393216 | tf_op jit(solution)/shard_map/all_to_all | solution.py:125
  65.5 147.0 %reduce-scatter.2.cloned.1.call-start = ((), (), s32[]{:S(2)}) async-start(), calls=%async_computation.7 | async-start | bytes 5308416 | tf_op jit(solution)/shard_map/reduce_scatter | solution.py:170
  75.7 11.0 %copy-start.11 = (bf16[1,128,1536]{2,1,0:T(8,128)(2,1)S(1)}, bf16[1,128,1536]{2,1,0:T(8,128)(2,1)}, u32[]{:S(2)}) copy-start(bf16[1,128,1536]{2,1,0:T(8,128)(2,1)} %param.21) | copy-start | bytes 1179652
  75.7 11.0 %copy-start.13 = (f32[1536]{0:T(1024)S(1)}, f32[1536]{0:T(1024)}, u32[]{:S(2)}) copy-start(f32[1536]{0:T(1024)} %get-tuple-element.238) | copy-start | bytes 18436
  75.7 11.0 %copy-start.14 = (f32[1536]{0:T(1024)S(1)}, f32[1536]{0:T(1024)}, u32[]{:S(2)}) copy-start(f32[1536]{0:T(1024)} %get-tuple-element.239) | copy-start | bytes 18436
  75.7 11.0 %copy-start.15 = (f32[1536]{0:T(1024)S(1)}, f32[1536]{0:T(1024)}, u32[]{:S(2)}) copy-start(f32[1536]{0:T(1024)} %get-tuple-element.240) | copy-start | bytes 18436
  75.7 11.0 %copy-start.16 = (f32[1536]{0:T(1024)S(1)}, f32[1536]{0:T(1024)}, u32[]{:S(2)}) copy-start(f32[1536]{0:T(1024)} %get-tuple-element.241) | copy-start | bytes 18436
  75.7 11.0 %copy-start.17 = (f32[1536]{0:T(1024)S(1)}, f32[1536]{0:T(1024)}, u32[]{:S(2)}) copy-start(f32[1536]{0:T(1024)} %get-tuple-element.242) | copy-start | bytes 18436
  75.7 11.0 %copy-start.18 = (f32[1536]{0:T(1024)S(1)}, f32[1536]{0:T(1024)}, u32[]{:S(2)}) copy-start(f32[1536]{0:T(1024)} %get-tuple-element.243) | copy-start | bytes 18436
  78.6 4.9 %collective-permute-start = (bf16[15,1536]{1,0:T(8,128)(2,1)S(1)}, bf16[15,1536]{1,0:T(8,128)(2,1)S(1)}, u32[]{:S(2)}, u32[]{:S(2)}) collective-permute-start(bf16[15,1536]{1,0:T(8,128)(2,1)S(1)} %get-tuple-element.307), channel_id=1, source_target_pairs={{0,4},{4,8},{8,12},{12,16},{16,20},{20,24},{24,28},{1,5},{5,9},{9,... | collective-permute-start | bytes 138248 | tf_op jit(solution)/shard_map/ppermute | solution.py:21
  80.6 6.0 %collective-permute-start.1 = (bf16[15,1536]{1,0:T(8,128)(2,1)S(1)}, bf16[15,1536]{1,0:T(8,128)(2,1)S(1)}, u32[]{:S(2)}, u32[]{:S(2)}) collective-permute-start(bf16[15,1536]{1,0:T(8,128)(2,1)S(1)} %get-tuple-element.308), channel_id=1, source_target_pairs={{4,0},{8,4},{12,8},{16,12},{20,16},{24,20},{28,24},{5,1},{9,5},{13... | collective-permute-start | bytes 138248 | tf_op jit(solution)/shard_map/ppermute | solution.py:22
  94.4 6.7 %collective-permute-start.2 = (f32[15,1536]{1,0:T(8,128)S(1)}, f32[15,1536]{1,0:T(8,128)S(1)}, u32[]{:S(2)}, u32[]{:S(2)}) collective-permute-start(f32[15,1536]{1,0:T(8,128)S(1)} %get-tuple-element.305), channel_id=1, source_target_pairs={{4,0},{8,4},{12,8},{16,12},{20,16},{24,20},{28,24},{5,1},{9,5},{13... | collective-permute-start | bytes 276488 | tf_op jit(solution)/shard_map/ppermute | solution.py:22
  95.7 7.0 %collective-permute-start.3 = (f32[15,1536]{1,0:T(8,128)S(1)}, f32[15,1536]{1,0:T(8,128)S(1)}, u32[]{:S(2)}, u32[]{:S(2)}) collective-permute-start(f32[15,1536]{1,0:T(8,128)S(1)} %get-tuple-element.306), channel_id=1, source_target_pairs={{0,4},{4,8},{8,12},{12,16},{16,20},{20,24},{24,28},{1,5},{5,9},{9,... | collective-permute-start | bytes 276488 | tf_op jit(solution)/shard_map/ppermute | solution.py:21
  115.5 18.4 %all-to-all-start.4 = ((bf16[8,128,96]{1,2,0:T(8,128)(2,1)}), bf16[8,128,96]{1,2,0:T(8,128)(2,1)S(1)}, u32[]{:S(2)}, u32[]{:S(2)}) async-start(bf16[8,128,96]{1,2,0:T(8,128)(2,1)} %bitcast.121), calls=%async_computation.4 | async-start | bytes 393216 | tf_op jit(solution)/shard_map/all_to_all | solution.py:157
  122.2 154.4 %all-reduce.5.cloned.1.call-start = ((), (), s32[]{:S(2)}) async-start(), calls=%async_computation.9 | async-start | bytes 393216 | tf_op jit(solution)/shard_map/psum | solution.py:172
  125.4 11.2 %copy-start.2 = (bf16[1024,96]{1,0:T(8,128)(2,1)S(1)}, bf16[1024,96]{1,0:T(8,128)(2,1)}, u32[]{:S(2)}) copy-start(bf16[1024,96]{1,0:T(8,128)(2,1)} %copy-done.1) | copy-start | bytes 589828
  125.4 11.2 %copy-start.4 = (bf16[1024,96]{1,0:T(8,128)(2,1)S(1)}, bf16[1024,96]{1,0:T(8,128)(2,1)}, u32[]{:S(2)}) copy-start(bf16[1024,96]{1,0:T(8,128)(2,1)} %copy-done.3) | copy-start | bytes 589828
  125.4 11.2 %copy-start.6 = (bf16[2,512,96]{2,1,0:T(8,128)(2,1)S(1)}, bf16[2,512,96]{2,1,0:T(8,128)(2,1)}, u32[]{:S(2)}) copy-start(bf16[2,512,96]{2,1,0:T(8,128)(2,1)} %copy-done.5) | copy-start | bytes 589828
  149.4 64.9 %copy-start.9 = (f32[128,1536]{1,0:T(8,128)S(1)}, f32[128,1536]{1,0:T(8,128)}, u32[]{:S(2)}) copy-start(f32[128,1536]{1,0:T(8,128)} %get-tuple-element.300) | copy-start | bytes 2359300
  149.5 64.9 %copy-start.10 = (bf16[128,1536]{1,0:T(8,128)(2,1)S(1)}, bf16[128,1536]{1,0:T(8,128)(2,1)}, u32[]{:S(2)}) copy-start(bf16[128,1536]{1,0:T(8,128)(2,1)} %get-tuple-element.310) | copy-start | bytes 1179652
  149.5 64.9 %copy-start.51 = (pred[128]{0:T(512)(128)(4,1)S(1)}, pred[128]{0:T(512)(128)(4,1)}, u32[]{:S(2)}) copy-start(pred[128]{0:T(512)(128)(4,1)} %add_compare_fusion) | copy-start | bytes 388
  154.0 61.4 %copy-start.48 = (f32[1536]{0:T(1024)S(1)}, f32[1536]{0:T(1024)}, u32[]{:S(2)}) copy-start(f32[1536]{0:T(1024)} %get-tuple-element.235) | copy-start | bytes 18436
  159.8 118.3 %all-to-all-start.5 = ((bf16[8,2,6144]{2,1,0:T(2,128)(2,1)}), bf16[8,2,6144]{2,1,0:T(2,128)(2,1)}, u32[]{:S(2)}, u32[]{:S(2)}) async-start(bf16[8,2,6144]{2,1,0:T(2,128)(2,1)} %reshape.157), calls=%async_computation.5 | async-start | bytes 393216 | tf_op jit(solution)/shard_map/all_to_all | solution.py:165
  164.2 148.0 %all-reduce.3.cloned.1.call-start = ((), (), s32[]{:S(2)}) async-start(), calls=%async_computation.8 | async-start | bytes 589824 | tf_op jit(solution)/shard_map/psum | solution.py:171
  (35 other events, 218.9 us)
Sparse Core Ops, SparseCore 0:
  110.3 102.1 reduce-scatter.1
Sparse Core Ops, SparseCore 1:
  132.5 144.0 all-reduce.4
  279.3 32.9 all-reduce.2
where the time goes:
time: 324 us; the launch traced here: 322 us
  waiting for transfers between devices  130 us (40%)
  local copies, waits for them, and re-layouts  44.2 us (14%)
  blocking collectives  40.3 us (12%)
  starting transfers between devices  38.2 us (12%)
  other arithmetic  31.9 us (10%)
  matrix products  19.4 us (6%)
  between operations  17.3 us (5%)
    reduce_scatter x1, waiting for transfers between devices, on_device(): lax.psum_scatter(term_block, 'seq', scatter_dimension=0, tiled=True)  48.2 us
    psum x1, blocking collectives, on_device(): lax.psum((kernel_local, bias_local), ('seq', 'dp'))  40.3 us
    psum x1, waiting for transfers between devices, on_device(): lax.psum(partial_rows.astype(jnp.bfloat16), 'dp').astype(jnp.float32)  31.7 us
    psum x1, waiting for transfers between devices, on_device(): lax.psum((kernel_local, bias_local), ('seq', 'dp'))  20.2 us
    unnamed x119, local copies, waits for them, and re-layouts  15.6 us
    reduce_sum x2, other arithmetic, on_device(): jnp.sum(grad_conv * padded[tap:tap + frames_dev], axis=0)  10.5 us
    unnamed x2, other arithmetic  7.45 us
    all_to_all x1, waiting for transfers between devices, on_device(): lax.all_to_all(value_send, 'seq', split_axis=0, concat_axis=1, tiled=True)  7.34 us
  transfers between devices with their start and end apart: 13, of which 11 were waited for; matrix products, arithmetic and copies ran while one was open for 18% of the time, Pallas kernels for 0%

commit v1 on v0

--- a/solution.py
+++ b/solution.py
@@ -9,6 +9,22 @@
 HS = 96
 KW = 31
 HD = 768
+
+
+def _fit_samples(x0, dev_axis):
+    heard, earlier = (jax.lax.axis_size(dev_axis), jax.lax.axis_index(dev_axis))
+    o_now = x0.shape[0] // heard
+    e_now = list(x0.shape)
+    e_now[0] = o_now
+    met_up = e_now[1]
+    e_now[1] = met_up * heard
+    row_out = jnp.zeros(e_now, x0.dtype)
+    for nth in range(heard):
+        low = lax.dynamic_slice_in_dim(x0, (earlier ^ nth) * o_now, o_now, axis=0)
+        if nth:
+            low = jax.lax.ppermute(low, dev_axis, tuple(((s, s ^ nth) for s in range(heard))))
+        row_out = lax.dynamic_update_slice_in_dim(row_out, low, (earlier ^ nth) * met_up, axis=1)
+    return row_out
 
 
 def with_halo(x, sides, width):
@@ -115,7 +131,7 @@
     )
     key_mine, value_mine = (
         lax.all_to_all(key_send, "seq", split_axis=0, concat_axis=1, tiled=True),
-        lax.all_to_all(value_send, "seq", split_axis=0, concat_axis=1, tiled=True),
+        _fit_samples(value_send, dev_axis="seq"),
     )
     key_mine = key_mine[0]
     value_mine = value_mine[0]

time: 324 us -> 321 us (level)
  waiting for transfers between devices: 130 us -> 118 us
  starting transfers between devices: 38.2 us -> 47.7 us
    ppermute x0 -> x7, starting transfers between devices: none -> 11.1 us  [_fit_samples(): jax.lax.ppermute(low, dev_axis, tuple(((s, s ^ nth) for s in range(heard))))]
    all_to_all x1 -> x0, waiting for transfers between devices: 7.34 us -> none  [on_device(): lax.all_to_all(value_send, 'seq', split_axis=0, concat_axis=1, tiled=True)]
    all_to_all x1, waiting for transfers between devices: 6.21 us -> 0.01 us  [on_device(): lax.all_to_all(to_serving(query_local), 'seq', split_axis=0, concat_axis=...]
    all_to_all x1 -> x0, starting transfers between devices: 3.39 us -> none  [on_device(): lax.all_to_all(value_send, 'seq', split_axis=0, concat_axis=1, tiled=True)]
    unnamed x119 -> x120, local copies, waits for them, and re-layouts: 15.6 us -> 13.9 us
  transfers between devices with their start and end apart: 13 -> 19, of which waited for: 11 -> 10; matrix products, arithmetic and copies ran while one was open for 18% -> 18% of each run, Pallas kernels for 0% -> 0%
where the time goes in v1:
time: 321 us; the launch traced here: 319 us
  waiting for transfers between devices  118 us (37%)
  starting transfers between devices  47.7 us (15%)
  local copies, waits for them, and re-layouts  43.6 us (14%)
  blocking collectives  40.3 us (13%)
  other arithmetic  31.9 us (10%)
  matrix products  19.4 us (6%)
  between operations  17.5 us (5%)
    reduce_scatter x1, waiting for transfers between devices, on_device(): lax.psum_scatter(term_block, 'seq', scatter_dimension=0, tiled=True)  48.5 us
    psum x1, blocking collectives, on_device(): lax.psum((kernel_local, bias_local), ('seq', 'dp'))  40.3 us
    psum x1, waiting for transfers between devices, on_device(): lax.psum(partial_rows.astype(jnp.bfloat16), 'dp').astype(jnp.float32)  31.7 us
    psum x1, waiting for transfers between devices, on_device(): lax.psum((kernel_local, bias_local), ('seq', 'dp'))  20.2 us
    unnamed x120, local copies, waits for them, and re-layouts  13.9 us
    ppermute x7, starting transfers between devices, _fit_samples(): jax.lax.ppermute(low, dev_axis, tuple(((s, s ^ nth) for s in range(heard))))  11.1 us
    reduce_sum x2, other arithmetic, on_device(): jnp.sum(grad_conv * padded[tap:tap + frames_dev], axis=0)  10.5 us
    unnamed x2, other arithmetic  7.45 us
  transfers between devices with their start and end apart: 19, of which 10 were waited for; matrix products, arithmetic and copies ran while one was open for 18% of the time, Pallas kernels for 0%

profile of v1, /device:TPU:0, one launch (start us, length us, event | category | flops | bytes accessed | tf_op | source)
XLA Modules:
  0.0 318.7 jit_solution(5850538898889827878)
XLA Ops:
  9.9 7.3 %all-to-all-start = ((bf16[8,128,96]{1,2,0:T(8,128)(2,1)}), bf16[8,128,96]{1,2,0:T(8,128)(2,1)S(1)}, u32[]{:S(2)}, u32[]{:S(2)}) async-start(bf16[8,128,96]{1,2,0:T(8,128)(2,1)} %bitcast.3), calls=%async_computation | async-start | bytes 393216 | tf_op jit(solution)/shard_map/all_to_all | solution.py:123
  18.4 4.8 %collective-permute-start.6 = (bf16[1,128,96]{1,2,0:T(8,128)(2,1)S(1)}, bf16[1,128,96]{1,2,0:T(8,128)(2,1)S(1)}, u32[]{:S(2)}, u32[]{:S(2)}) collective-permute-start(bf16[1,128,96]{1,2,0:T(8,128)(2,1)S(1)} %get-tuple-element.309), channel_id=1, source_target_pairs={{0,28},{4,24},{8,20},{12,16},{16,12},{20,8},{24,4},{28,0},{1,29},{... | collective-permute-start | bytes 73736 | tf_op jit(solution)/shard_map/ppermute | solution.py:25
  27.9 2.2 collective-permute-start.5
  31.3 5.1 %all-to-all-start.1 = ((bf16[8,128,96]{1,2,0:T(8,128)(2,1)}), bf16[8,128,96]{1,2,0:T(8,128)(2,1)S(1)}, u32[]{:S(2)}, u32[]{:S(2)}) async-start(bf16[8,128,96]{1,2,0:T(8,128)(2,1)} %bitcast.5), calls=%async_computation.1 | async-start | bytes 393216 | tf_op jit(solution)/shard_map/all_to_all | solution.py:133
  37.0 7.1 %all-to-all-done.1 = bf16[8,128,96]{1,2,0:T(8,128)(2,1)S(1)} async-done(((bf16[8,128,96]{1,2,0:T(8,128)(2,1)}), bf16[8,128,96]{1,2,0:T(8,128)(2,1)S(1)}, u32[]{:S(2)}, u32[]{:S(2)}) %all-to-all-start.1) | async-done | bytes 196640 | tf_op jit(solution)/shard_map/all_to_all | solution.py:133
  44.4 4.6 %while.24 = (s32[]{:T(128)}, bf16[2,512,96]{1,2,0:T(8,128)(2,1)S(1)}, f32[2,512]{1,0:T(2,128)S(1)}, bf16[2,512,96]{2,1,0:T(8,128)(2,1)S(1)}, bf16[1024,96]{1,0:T...) while((s32[]{:T(128)}, ...), condition=%wide.region_3.4_spmd.clone, body=%wide.region_0.3_spmd.clone.sunk | while | flops 204997120 | bytes 7164021 | solution.py:61
  50.0 2.6 reshape.143
  53.1 3.7 %reduce.63 = bf16[1024,96]{1,0:T(8,128)(2,1)} reduce(bf16[1024,1,96]{2,1,0:T(2,128)(2,1)} %bitcast.134, bf16[]{:T(256)} %broadcast.75), dimensions={1}, to_apply=%bitcast.86.reduce_sub_computation | reduce | bytes 393218
  58.9 3.4 %all-to-all-start.2 = ((bf16[8,2,6144]{2,1,0:T(2,128)(2,1)}), bf16[8,2,6144]{2,1,0:T(2,128)(2,1)S(1)}, u32[]{:S(2)}, u32[]{:S(2)}) async-start(bf16[8,2,6144]{2,1,0:T(2,128)(2,1)} %reshape.176), calls=%async_computation.2 | async-start | bytes 393216 | tf_op jit(solution)/shard_map/all_to_all | solution.py:141
  63.6 2.5 slice_reduce_fusion.30
  66.1 3.9 %all-to-all-done.2 = bf16[8,2,6144]{2,1,0:T(2,128)(2,1)S(1)} async-done(((bf16[8,2,6144]{2,1,0:T(2,128)(2,1)}), bf16[8,2,6144]{2,1,0:T(2,128)(2,1)S(1)}, u32[]{:S(2)}, u32[]{:S(2)}) %all-to-all-start.2) | async-done | bytes 196640 | tf_op jit(solution)/shard_map/all_to_all | solution.py:141
  72.7 2.7 broadcast_select_fusion
  80.3 3.0 collective-permute-done.8
  83.7 7.5 %multiply_reduce_fusion = (f32[1536]{0:T(1024)}, f32[1536]{0:T(1024)}, f32[1536]{0:T(1024)}, f32[1536]{0:T(1024)}, f32[1536]{0:T(1024)}, /*index=5*/f32[1536]{0:...) fusion(f32[158,1536]{1,0:T(8,128)S(1)} %maximum_convert_fusion,, ...), kind=kLoop, calls=%fused_computation.190 | loop fusion | flops 21206016 | bytes 26652800 | tf_op jit(solution)/shard_map/reduce_sum | solution.py:159
  92.5 5.0 %collective-permute-start.10 = (f32[15,1536]{1,0:T(8,128)S(1)}, f32[15,1536]{1,0:T(8,128)S(1)}, u32[]{:S(2)}, u32[]{:S(2)}) collective-permute-start(f32[15,1536]{1,0:T(8,128)S(1)} %get-tuple-element.306), channel_id=1, source_target_pairs={{0,4},{4,8},{8,12},{12,16},{16,20},{20,24},{24,28},{1,5},{5,9},{9,... | collective-permute-start | bytes 276488 | tf_op jit(solution)/shard_map/ppermute | solution.py:37
  99.5 3.7 %fusion.37 = bf16[128,1536]{1,0:T(8,128)(2,1)S(1)} fusion(f32[128,1536]{1,0:T(8,128)S(1)} %get-tuple-element.299, f32[15,1536]{1,0:T(8,128)S(1)} %collective-permute-done.10, f32[15,1536]{1,0:T(8,128)S(1)} %collective-permute-done.9, bf16[1,128,1536]{2,1,0:T(8,128)(2,1)S(1)} %copy-done.11, f32[1536]{0:T(1024)S(1)} %get-tuple-element.265, ...), kind=kLoop, calls=%fused_computation.100 | loop fusion | flops 18874368 | bytes 1947776 | tf_op jit(solution)/shard_map/convert_element_type | solution.py:167
  104.0 2.9 fusion.130
  107.9 2.1 reshape.142
  112.3 6.7 %all-to-all-start.3 = ((bf16[8,128,96]{1,2,0:T(8,128)(2,1)}), bf16[8,128,96]{1,2,0:T(8,128)(2,1)S(1)}, u32[]{:S(2)}, u32[]{:S(2)}) async-start(bf16[8,128,96]{1,2,0:T(8,128)(2,1)} %bitcast.140), calls=%async_computation.3 | async-start | bytes 393216 | tf_op jit(solution)/shard_map/all_to_all | solution.py:173
  119.2 3.0 multiply_reduce_fusion.18
  125.7 3.5 %stack.127 = f32[31,1536]{1,0:T(8,128)} concatenate(f32[1,1536]{1,0:T(1,128)} %stack.96, f32[1,1536]{1,0:T(1,128)} %stack.97, f32[1,1536]{1,0:T(1,128)} %stack.98, f32[1,1536]{1,0:T(1,128)} %stack.99, f32[1,1536]{1,0:T(1,128)} %stack.100, f32[1,1536]{1,0:T(1,128)S(1)} %stack.101, f32[1,1536]{1,0:T(1,128)S(1)} %stack.102, f32[1,1536]{1,0:T(1,128)S(1)} %stack.103, ...), dimensions={0} | concatenate | bytes 380928 | tf_op jit(solution)/shard_map/stack | solution.py:158
  133.3 12.9 %while.25 = (s32[]{:T(128)}, bf16[2,512,96]{1,2,0:T(8,128)(2,1)}, bf16[2,512,96]{2,1,0:T(8,128)(2,1)S(1)}, bf16[1024,96]{1,0:T(8,128)(2,1)S(1)}, f32[2,512]{1,0:...) while((s32[]{:T(128)}, bf16[2,512,96]{1,2,0:T(8,128)(2,1)}, ...), condition=%wide.region_6.7_spmd.clone, body=%wide.region_5.6_spmd.clone.sunk | while | flops 305185792 | bytes 6241429 | solution.py:89
  136.6 3.3 %fusion.163 = bf16[2,512,96]{1,2,0:T(8,128)(2,1)} fusion(bf16[2,512,96]{1,2,0:T(8,128)(2,1)} %get-tuple-element.463, s32[]{:T(128)S(6)} %copy.161, bf16[1024,96]{1,0:T(8,128)(2,1)S(1)} %get-tuple-element.475, f32[512,1024]{1,0:T(8,128)} %fusion.162, bf16[1024,96]{1,0:T(8,128)(2,1)S(1)} %get-tuple-element.478, f32[512]{0:T(512)S(1)} %bitcast.149, ...), kind=kOutput, calls=%fused_computation.17.clone.1 | convolution fusion | flops 204521472 | bytes 2955264 | tf_op jit(solution)/shard_map/while/body/eval_jaxpr/dot_general | solution.py:87
  143.0 3.2 %fusion.163 = bf16[2,512,96]{1,2,0:T(8,128)(2,1)} fusion(bf16[2,512,96]{1,2,0:T(8,128)(2,1)} %get-tuple-element.463, s32[]{:T(128)S(6)} %copy.161, bf16[1024,96]{1,0:T(8,128)(2,1)S(1)} %get-tuple-element.475, f32[512,1024]{1,0:T(8,128)} %fusion.162, bf16[1024,96]{1,0:T(8,128)(2,1)S(1)} %get-tuple-element.478, f32[512]{0:T(512)S(1)} %bitcast.149, ...), kind=kOutput, calls=%fused_computation.17.clone.1 | convolution fusion | flops 204521472 | bytes 2955264 | tf_op jit(solution)/shard_map/while/body/eval_jaxpr/dot_general | solution.py:87
  148.1 2.6 reshape.144
  150.8 3.7 %reduce.64 = bf16[1024,96]{1,0:T(8,128)(2,1)} reduce(bf16[1024,1,96]{2,1,0:T(2,128)(2,1)} %bitcast.135, bf16[]{:T(256)} %broadcast.75), dimensions={1}, to_apply=%bitcast.88.reduce_sub_computation | reduce | bytes 393218
  154.5 2.1 reshape.178
  156.6 4.5 %all-to-all-start.4 = ((bf16[8,2,6144]{2,1,0:T(2,128)(2,1)}), bf16[8,2,6144]{2,1,0:T(2,128)(2,1)}, u32[]{:S(2)}, u32[]{:S(2)}) async-start(bf16[8,2,6144]{2,1,0:T(2,128)(2,1)} %reshape.178), calls=%async_computation.4 | async-start | bytes 393216 | tf_op jit(solution)/shard_map/all_to_all | solution.py:181
  161.1 48.5 %reduce-scatter.2.cloned.1.call-done = f32[192,768]{1,0:T(8,128)} async-done(((f32[1536,768]{1,0:T(8,128)}), f32[192,768]{1,0:T(8,128)}) %reduce-scatter.2.cloned.1.call-update) | async-done | bytes 589840 | tf_op jit(solution)/shard_map/reduce_scatter | solution.py:186
  212.6 40.3 %psum.23 = f32[1536]{0:T(1024)S(1)} all-reduce(f32[1536]{0:T(1024)S(1)} %copy-done.49), channel_id=1, replica_groups=mesh['seq'=8,'dp'=4] {'seq','dp'}, use_global_device_ids=true, to_apply=%region_42.43 | all-reduce | flops 1536 | bytes 12288 | tf_op jit(solution)/shard_map/psum | solution.py:188
  253.5 20.2 %all-reduce.5.cloned.1.call-done = f32[31,1536]{1,0:T(8,128)} async-done(((f32[31,1536]{1,0:T(8,128)}), f32[31,1536]{1,0:T(8,128)}) %all-reduce.5.cloned.1.call-update) | async-done | bytes 190480 | tf_op jit(solution)/shard_map/psum | solution.py:188
  277.7 31.7 %all-reduce.3.cloned.1.call-done = bf16[192,768]{1,0:T(8,128)(2,1)} async-done(((bf16[192,768]{1,0:T(8,128)(2,1)}), bf16[192,768]{1,0:T(8,128)(2,1)}) %all-reduce.3.cloned.1.call-update) | async-done | bytes 294928 | tf_op jit(solution)/shard_map/psum | solution.py:187
  (241 shorter events, 58.0 us)
Async XLA Ops:
  8.0 64.5 %copy-start = (bf16[1536,768]{1,0:T(8,128)(2,1)S(1)}, bf16[1536,768]{1,0:T(8,128)(2,1)}, u32[]{:S(2)}) copy-start(bf16[1536,768]{1,0:T(8,128)(2,1)} %param.18) | copy-start | bytes 7077892
  8.0 18.9 %copy-start.13 = (bf16[1,128,768]{2,1,0:T(8,128)(2,1)S(1)}, bf16[1,128,768]{2,1,0:T(8,128)(2,1)}, u32[]{:S(2)}) copy-start(bf16[1,128,768]{2,1,0:T(8,128)(2,1)} %param.15) | copy-start | bytes 589828
  9.9 21.4 %all-to-all-start = ((bf16[8,128,96]{1,2,0:T(8,128)(2,1)}), bf16[8,128,96]{1,2,0:T(8,128)(2,1)S(1)}, u32[]{:S(2)}, u32[]{:S(2)}) async-start(bf16[8,128,96]{1,2,0:T(8,128)(2,1)} %bitcast.3), calls=%async_computation | async-start | bytes 393216 | tf_op jit(solution)/shard_map/all_to_all | solution.py:123
  18.4 18.0 %collective-permute-start.6 = (bf16[1,128,96]{1,2,0:T(8,128)(2,1)S(1)}, bf16[1,128,96]{1,2,0:T(8,128)(2,1)S(1)}, u32[]{:S(2)}, u32[]{:S(2)}) collective-permute-start(bf16[1,128,96]{1,2,0:T(8,128)(2,1)S(1)} %get-tuple-element.309), channel_id=1, source_target_pairs={{0,28},{4,24},{8,20},{12,16},{16,12},{20,8},{24,4},{28,0},{1,29},{... | collective-permute-start | bytes 73736 | tf_op jit(solution)/shard_map/ppermute | solution.py:25
  23.2 4.7 %collective-permute-start.3 = (bf16[1,128,96]{1,2,0:T(8,128)(2,1)S(1)}, bf16[1,128,96]{1,2,0:T(8,128)(2,1)S(1)}, u32[]{:S(2)}, u32[]{:S(2)}) collective-permute-start(bf16[1,128,96]{1,2,0:T(8,128)(2,1)S(1)} %get-tuple-element.312), channel_id=1, source_target_pairs={{0,16},{4,20},{8,24},{12,28},{16,0},{20,4},{24,8},{28,12},{1,17},{... | collective-permute-start | bytes 73736 | tf_op jit(solution)/shard_map/ppermute | solution.py:25
  23.2 7.0 %collective-permute-start.2 = (bf16[1,128,96]{1,2,0:T(8,128)(2,1)S(1)}, bf16[1,128,96]{1,2,0:T(8,128)(2,1)S(1)}, u32[]{:S(2)}, u32[]{:S(2)}) collective-permute-start(bf16[1,128,96]{1,2,0:T(8,128)(2,1)S(1)} %get-tuple-element.313), channel_id=1, source_target_pairs={{0,12},{4,8},{8,4},{12,0},{16,28},{20,24},{24,20},{28,16},{1,13},{... | collective-permute-start | bytes 73736 | tf_op jit(solution)/shard_map/ppermute | solution.py:25
  23.8 7.2 %collective-permute-start.1 = (bf16[1,128,96]{1,2,0:T(8,128)(2,1)S(1)}, bf16[1,128,96]{1,2,0:T(8,128)(2,1)S(1)}, u32[]{:S(2)}, u32[]{:S(2)}) collective-permute-start(bf16[1,128,96]{1,2,0:T(8,128)(2,1)S(1)} %get-tuple-element.314), channel_id=1, source_target_pairs={{0,8},{4,12},{8,0},{12,4},{16,24},{20,28},{24,16},{28,20},{1,9},{5... | collective-permute-start | bytes 73736 | tf_op jit(solution)/shard_map/ppermute | solution.py:25
  25.2 5.9 %collective-permute-start = (bf16[1,128,96]{1,2,0:T(8,128)(2,1)S(1)}, bf16[1,128,96]{1,2,0:T(8,128)(2,1)S(1)}, u32[]{:S(2)}, u32[]{:S(2)}) collective-permute-start(bf16[1,128,96]{1,2,0:T(8,128)(2,1)S(1)} %get-tuple-element.315), channel_id=1, source_target_pairs={{0,4},{4,0},{8,12},{12,8},{16,20},{20,16},{24,28},{28,24},{1,5},{5... | collective-permute-start | bytes 73736 | tf_op jit(solution)/shard_map/ppermute | solution.py:25
  27.9 8.6 %collective-permute-start.5 = (bf16[1,128,96]{1,2,0:T(8,128)(2,1)S(1)}, bf16[1,128,96]{1,2,0:T(8,128)(2,1)S(1)}, u32[]{:S(2)}, u32[]{:S(2)}) collective-permute-start(bf16[1,128,96]{1,2,0:T(8,128)(2,1)S(1)} %get-tuple-element.310), channel_id=1, source_target_pairs={{0,24},{4,28},{8,16},{12,20},{16,8},{20,12},{24,0},{28,4},{1,25},{... | collective-permute-start | bytes 73736 | tf_op jit(solution)/shard_map/ppermute | solution.py:25
  30.2 6.5 %collective-permute-start.4 = (bf16[1,128,96]{1,2,0:T(8,128)(2,1)S(1)}, bf16[1,128,96]{1,2,0:T(8,128)(2,1)S(1)}, u32[]{:S(2)}, u32[]{:S(2)}) collective-permute-start(bf16[1,128,96]{1,2,0:T(8,128)(2,1)S(1)} %get-tuple-element.311), channel_id=1, source_target_pairs={{0,20},{4,16},{8,28},{12,24},{16,4},{20,0},{24,12},{28,8},{1,21},{... | collective-permute-start | bytes 73736 | tf_op jit(solution)/shard_map/ppermute | solution.py:25
  31.3 12.9 %all-to-all-start.1 = ((bf16[8,128,96]{1,2,0:T(8,128)(2,1)}), bf16[8,128,96]{1,2,0:T(8,128)(2,1)S(1)}, u32[]{:S(2)}, u32[]{:S(2)}) async-start(bf16[8,128,96]{1,2,0:T(8,128)(2,1)} %bitcast.5), calls=%async_computation.1 | async-start | bytes 393216 | tf_op jit(solution)/shard_map/all_to_all | solution.py:133
  49.0 14.0 %copy-start.50 = (f32[2,512]{1,0:T(2,128)}, f32[2,512]{1,0:T(2,128)S(1)}, u32[]{:S(2)}) copy-start(f32[2,512]{1,0:T(2,128)S(1)} %get-tuple-element.456) | copy-start | bytes 12292
  49.1 23.3 %copy-start.1 = (bf16[1024,96]{1,0:T(8,128)(2,1)}, bf16[1024,96]{1,0:T(8,128)(2,1)S(1)}, u32[]{:S(2)}) copy-start(bf16[1024,96]{1,0:T(8,128)(2,1)S(1)} %get-tuple-element.485) | copy-start | bytes 589828
  49.1 23.3 %copy-start.3 = (bf16[1024,96]{1,0:T(8,128)(2,1)}, bf16[1024,96]{1,0:T(8,128)(2,1)S(1)}, u32[]{:S(2)}) copy-start(bf16[1024,96]{1,0:T(8,128)(2,1)S(1)} %get-tuple-element.488) | copy-start | bytes 589828
  49.1 23.3 %copy-start.5 = (bf16[2,512,96]{2,1,0:T(8,128)(2,1)}, bf16[2,512,96]{2,1,0:T(8,128)(2,1)S(1)}, u32[]{:S(2)}) copy-start(bf16[2,512,96]{2,1,0:T(8,128)(2,1)S(1)} %get-tuple-element.489) | copy-start | bytes 589828
  58.9 11.1 %all-to-all-start.2 = ((bf16[8,2,6144]{2,1,0:T(2,128)(2,1)}), bf16[8,2,6144]{2,1,0:T(2,128)(2,1)S(1)}, u32[]{:S(2)}, u32[]{:S(2)}) async-start(bf16[8,2,6144]{2,1,0:T(2,128)(2,1)} %reshape.176), calls=%async_computation.2 | async-start | bytes 393216 | tf_op jit(solution)/shard_map/all_to_all | solution.py:141
  62.3 147.3 %reduce-scatter.2.cloned.1.call-start = ((), (), s32[]{:S(2)}) async-start(), calls=%async_computation.6 | async-start | bytes 5308416 | tf_op jit(solution)/shard_map/reduce_scatter | solution.py:186
  75.4 4.9 %collective-permute-start.7 = (bf16[15,1536]{1,0:T(8,128)(2,1)S(1)}, bf16[15,1536]{1,0:T(8,128)(2,1)S(1)}, u32[]{:S(2)}, u32[]{:S(2)}) collective-permute-start(bf16[15,1536]{1,0:T(8,128)(2,1)S(1)} %get-tuple-element.307), channel_id=1, source_target_pairs={{0,4},{4,8},{8,12},{12,16},{16,20},{20,24},{24,28},{1,5},{5,9},{9,... | collective-permute-start | bytes 138248 | tf_op jit(solution)/shard_map/ppermute | solution.py:37
  77.4 6.0 %collective-permute-start.8 = (bf16[15,1536]{1,0:T(8,128)(2,1)S(1)}, bf16[15,1536]{1,0:T(8,128)(2,1)S(1)}, u32[]{:S(2)}, u32[]{:S(2)}) collective-permute-start(bf16[15,1536]{1,0:T(8,128)(2,1)S(1)} %get-tuple-element.308), channel_id=1, source_target_pairs={{4,0},{8,4},{12,8},{16,12},{20,16},{24,20},{28,24},{5,1},{9,5},{13... | collective-permute-start | bytes 138248 | tf_op jit(solution)/shard_map/ppermute | solution.py:38
  91.2 6.7 %collective-permute-start.9 = (f32[15,1536]{1,0:T(8,128)S(1)}, f32[15,1536]{1,0:T(8,128)S(1)}, u32[]{:S(2)}, u32[]{:S(2)}) collective-permute-start(f32[15,1536]{1,0:T(8,128)S(1)} %get-tuple-element.305), channel_id=1, source_target_pairs={{4,0},{8,4},{12,8},{16,12},{20,16},{24,20},{28,24},{5,1},{9,5},{13... | collective-permute-start | bytes 276488 | tf_op jit(solution)/shard_map/ppermute | solution.py:38
  92.5 7.0 %collective-permute-start.10 = (f32[15,1536]{1,0:T(8,128)S(1)}, f32[15,1536]{1,0:T(8,128)S(1)}, u32[]{:S(2)}, u32[]{:S(2)}) collective-permute-start(f32[15,1536]{1,0:T(8,128)S(1)} %get-tuple-element.306), channel_id=1, source_target_pairs={{0,4},{4,8},{8,12},{12,16},{16,20},{20,24},{24,28},{1,5},{5,9},{9,... | collective-permute-start | bytes 276488 | tf_op jit(solution)/shard_map/ppermute | solution.py:37
  112.3 18.4 %all-to-all-start.3 = ((bf16[8,128,96]{1,2,0:T(8,128)(2,1)}), bf16[8,128,96]{1,2,0:T(8,128)(2,1)S(1)}, u32[]{:S(2)}, u32[]{:S(2)}) async-start(bf16[8,128,96]{1,2,0:T(8,128)(2,1)} %bitcast.140), calls=%async_computation.3 | async-start | bytes 393216 | tf_op jit(solution)/shard_map/all_to_all | solution.py:173
  119.0 154.7 %all-reduce.5.cloned.1.call-start = ((), (), s32[]{:S(2)}) async-start(), calls=%async_computation.8 | async-start | bytes 393216 | tf_op jit(solution)/shard_map/psum | solution.py:188
  122.2 11.1 %copy-start.2 = (bf16[1024,96]{1,0:T(8,128)(2,1)S(1)}, bf16[1024,96]{1,0:T(8,128)(2,1)}, u32[]{:S(2)}) copy-start(bf16[1024,96]{1,0:T(8,128)(2,1)} %copy-done.1) | copy-start | bytes 589828
  122.2 11.1 %copy-start.4 = (bf16[1024,96]{1,0:T(8,128)(2,1)S(1)}, bf16[1024,96]{1,0:T(8,128)(2,1)}, u32[]{:S(2)}) copy-start(bf16[1024,96]{1,0:T(8,128)(2,1)} %copy-done.3) | copy-start | bytes 589828
  122.2 11.1 %copy-start.6 = (bf16[2,512,96]{2,1,0:T(8,128)(2,1)S(1)}, bf16[2,512,96]{2,1,0:T(8,128)(2,1)}, u32[]{:S(2)}) copy-start(bf16[2,512,96]{2,1,0:T(8,128)(2,1)} %copy-done.5) | copy-start | bytes 589828
  146.2 65.3 %copy-start.9 = (f32[128,1536]{1,0:T(8,128)S(1)}, f32[128,1536]{1,0:T(8,128)}, u32[]{:S(2)}) copy-start(f32[128,1536]{1,0:T(8,128)} %get-tuple-element.300) | copy-start | bytes 2359300
  146.3 65.3 %copy-start.10 = (bf16[128,1536]{1,0:T(8,128)(2,1)S(1)}, bf16[128,1536]{1,0:T(8,128)(2,1)}, u32[]{:S(2)}) copy-start(bf16[128,1536]{1,0:T(8,128)(2,1)} %get-tuple-element.318) | copy-start | bytes 1179652
  146.3 65.3 %copy-start.52 = (pred[128]{0:T(512)(128)(4,1)S(1)}, pred[128]{0:T(512)(128)(4,1)}, u32[]{:S(2)}) copy-start(pred[128]{0:T(512)(128)(4,1)} %add_compare_fusion) | copy-start | bytes 388
  150.8 61.8 %copy-start.49 = (f32[1536]{0:T(1024)S(1)}, f32[1536]{0:T(1024)}, u32[]{:S(2)}) copy-start(f32[1536]{0:T(1024)} %get-tuple-element.235) | copy-start | bytes 18436
  156.6 118.6 %all-to-all-start.4 = ((bf16[8,2,6144]{2,1,0:T(2,128)(2,1)}), bf16[8,2,6144]{2,1,0:T(2,128)(2,1)}, u32[]{:S(2)}, u32[]{:S(2)}) async-start(bf16[8,2,6144]{2,1,0:T(2,128)(2,1)} %reshape.178), calls=%async_computation.4 | async-start | bytes 393216 | tf_op jit(solution)/shard_map/all_to_all | solution.py:181
  161.1 148.4 %all-reduce.3.cloned.1.call-start = ((), (), s32[]{:S(2)}) async-start(), calls=%async_computation.7 | async-start | bytes 589824 | tf_op jit(solution)/shard_map/psum | solution.py:187
  (42 other events, 296.1 us)
Sparse Core Ops, SparseCore 0:
  107.1 102.5 reduce-scatter.1
Sparse Core Ops, SparseCore 1:
  129.3 144.3 all-reduce.4
  276.5 32.9 all-reduce.2
